TPU v7x, 256 devices: a whole 4x4x8 slice. The times are simulated.
256 devices in a mesh: seq: 32 (over y, z), head: 8 (over x, core).
Axes of the slice: x: 4, y: 4, z: 8, core: 2. Of those that a mesh axis runs over, the one named last changes fastest.
Arguments:
- inputs: bfloat16 [8192, 8192], P('seq'), may hold values from -6 to 6
- w_value: bfloat16 [8192, 4096], P('seq', 'head'), may hold values from -0.0625 to 0.0625
- log_decay: float32 [8192, 64], P('seq', 'head'), may hold values from -1 to 0
- b_proj: bfloat16 [8192, 128], P('seq'), may hold values from -0.5 to 0.5
- c_proj: bfloat16 [8192, 128], P('seq'), may hold values from -0.5 to 0.5
- grad_out: bfloat16 [8192, 4096], P('seq', 'head'), may hold values from -6 to 6
Outputs:
- grad_input: bfloat16 [8192, 8192], P('seq', 'head')
- grad_weight: float32 [8192, 4096], P('seq', 'head')
- grad_b: float32 [8192, 128], P('seq')
- grad_c: float32 [8192, 128], P('seq')
All inputs are finite; a program needn't handle non-finite values.
Results may differ from a plain program's by a relative error of at most 0.027.
Values may be sent and summed in bfloat16 or wider, within the bound.
A program may use at most 128 MiB of HBM per device.

v0:
```python
import jax
import jax.numpy as jnp
from jax import lax
from jax.sharding import PartitionSpec as P

SPAN = 256
HIGH = lax.Precision.HIGHEST


def carried_in(array, axis, combine, identity, reverse):
    length, index = (lax.axis_size(axis), lax.axis_index(axis))
    everything = jax.tree.map(
        lambda part, kind: lax.all_gather(part.astype(kind), axis),
        array,
        (jnp.bfloat16, jnp.bfloat16),
    )
    start = jax.tree.map(
        lambda part, zero: jnp.broadcast_to(jnp.asarray(zero, part.dtype), part.shape),
        array,
        identity,
    )

    def lap(k, before):
        at = length - 1 - k if reverse else k
        reached = at > index if reverse else at < index
        new = combine(
            before, jax.tree.map(lambda part, own: part[at].astype(own.dtype), everything, array)
        )
        return jax.tree.map(lambda a, b: jnp.where(reached, a, b), new, before)

    return lax.fori_loop(0, length, lap, start)


def link(earlier, later):
    return (earlier[0] * later[0], later[0][:, None, None] * earlier[1] + later[1])


def advance_once(carried, item):
    decay, local = item
    return (decay[:, None, None] * carried + local, carried)


def per_device(inputs, w_value, log_decay, b_proj, c_proj, grad_out):
    steps = inputs.shape[0]
    heads = log_decay.shape[1]
    columns = grad_out.shape[1]
    depth = columns // heads
    states = b_proj.shape[1]
    blocks = steps // SPAN
    w_full = lax.all_gather(w_value, "seq", axis=0, tiled=True)
    values = jnp.dot(inputs, w_full, preferred_element_type=jnp.float32).astype(jnp.bfloat16)
    xs = values.astype(jnp.float32).reshape(blocks, SPAN, heads, depth)
    dys = grad_out.astype(jnp.float32).reshape(blocks, SPAN, heads, depth)
    bs = b_proj.astype(jnp.float32).reshape(blocks, SPAN, states)
    cs = c_proj.astype(jnp.float32).reshape(blocks, SPAN, states)
    cum_log = jnp.cumsum(log_decay.reshape(blocks, SPAN, heads), axis=1)
    totals = cum_log[:, -1]
    grow = jnp.exp(cum_log)
    shrink = jnp.exp(totals[:, None] - cum_log)
    cum_heads = jnp.swapaxes(cum_log, 1, 2)
    rows = lax.broadcasted_iota(jnp.int32, (SPAN, SPAN), 0)
    cols = lax.broadcasted_iota(jnp.int32, (SPAN, SPAN), 1)
    lower = (rows >= cols)[None, None]
    diff = cum_heads[:, :, :, None] - cum_heads[:, :, None, :]
    decay_mat = jnp.exp(jnp.where(lower, diff, -jnp.inf))
    cross = jnp.einsum("kthp,kjhp->khtj", dys, xs, precision=HIGH)
    mixed = decay_mat * cross
    scores = jnp.einsum("ktn,kjn->ktj", cs, bs, precision=HIGH)
    span_decay = jnp.exp(totals)
    dev_decay = jnp.exp(jnp.sum(totals, axis=0))
    zero_state = jnp.zeros((heads, depth, states), jnp.float32)
    identity_matrix = (jnp.ones_like(dev_decay), zero_state)
    local_end = jnp.einsum("kjhp,kjh,kjn->khpn", xs, shrink, bs, precision=HIGH)
    dev_state, before = lax.scan(advance_once, zero_state, (span_decay, local_end))
    incoming = carried_in((dev_decay, dev_state), "seq", link, identity_matrix, False)[1]
    lead = jnp.exp(jnp.cumsum(totals, axis=0) - totals)
    state_in = before + lead[:, :, None, None] * incoming[None]
    grad_c = jnp.einsum("kthp,khpn,kth->ktn", dys, state_in, grow, precision=HIGH)
    grad_c = grad_c + jnp.einsum("khtj,kjn->ktn", mixed, bs, precision=HIGH)
    local_back = jnp.einsum("kthp,kth,ktn->khpn", dys, grow, cs, precision=HIGH)
    dev_back, after = lax.scan(advance_once, zero_state, (span_decay, local_back), reverse=True)
    incoming_back = carried_in((dev_decay, dev_back), "seq", link, identity_matrix, True)[1]
    trail = jnp.exp(jnp.sum(totals, axis=0)[None] - jnp.cumsum(totals, axis=0))
    grad_in = after + trail[:, :, None, None] * incoming_back[None]
    grad_vals = jnp.einsum("khst,kst,kshp->kthp", decay_mat, scores, dys, precision=HIGH)
    grad_vals = grad_vals + jnp.einsum("khpn,ktn,kth->kthp", grad_in, bs, shrink, precision=HIGH)
    grad_b = jnp.einsum("khst,ksn->ktn", mixed, cs, precision=HIGH)
    grad_b = grad_b + jnp.einsum("kthp,khpn,kth->ktn", xs, grad_in, shrink, precision=HIGH)
    grad_values = grad_vals.reshape(steps, columns).astype(jnp.bfloat16)
    grad_b, grad_c = (
        lax.psum(grad_b.reshape(steps, states).astype(jnp.bfloat16), "head").astype(jnp.float32),
        lax.psum(grad_c.reshape(steps, states).astype(jnp.bfloat16), "head").astype(jnp.float32),
    )
    term = lax.dot_general(
        grad_values, w_full, (((1,), (1,)), ((), ())), preferred_element_type=jnp.float32
    )
    grad_input = lax.psum_scatter(
        term.astype(jnp.bfloat16), "head", scatter_dimension=1, tiled=True
    )
    grad_weight = lax.psum_scatter(
        lax.dot_general(
            inputs, grad_values, (((0,), (0,)), ((), ())), preferred_element_type=jnp.float32
        ).astype(jnp.bfloat16),
        "seq",
        scatter_dimension=0,
        tiled=True,
    ).astype(jnp.float32)
    return (grad_input, grad_weight, grad_b, grad_c)


def solution(mesh):
    placed = (
        P("seq", None),
        P("seq", "head"),
        P("seq", "head"),
        P("seq", None),
        P("seq", None),
        P("seq", "head"),
    )
    return jax.shard_map(
        per_device,
        mesh=mesh,
        in_specs=placed,
        out_specs=(P("seq", "head"), P("seq", "head"), P("seq", None), P("seq", None)),
        check_vma=False,
    )
```

profile of v0, /device:TPU:8, one launch (start us, length us, event | category | flops | bytes accessed | tf_op | source)
XLA Modules:
  0.0 655.9 jit_solution(10136107935495648219)
XLA Ops:
  8.0 1.3 reduce-window.6
  9.4 1.1 copy.32
  10.8 1.9 fusion.18
  13.0 41.5 %all-gather = bf16[32,1,8]{2,1,0:T(2,128)(2,1)S(1)} all-gather(bf16[1,1,8]{2,1,0:T(2,128)(2,1)S(1)} %copy.34), channel_id=2, replica_groups=mesh['seq'=32,'head'=8] {'seq'}, dimensions={0}, use_global_device_ids=true | all-gather | bytes 528 | tf_op jit(solution)/shard_map/all_gather | solution.py:13
  54.6 1.0 fusion.43
  55.7 54.8 %all-gather.7.cloned.1.call-done = bf16[8192,512]{1,0:T(8,128)(2,1)} async-done(((bf16[256,512]{1,0:T(8,128)(2,1)}), bf16[8192,512]{1,0:T(8,128)(2,1)}) %all-gather.7.cloned.1.call-update) | async-done | bytes 8388624 | tf_op jit(solution)/shard_map/all_gather | solution.py:50
  110.5 7.0 %convolution_convert_fusion.2 = bf16[256,512]{1,0:T(8,128)(2,1)S(1)} fusion(bf16[256,8192]{1,0:T(8,128)(2,1)} %param.10, bf16[8192,512]{1,0:T(8,128)(2,1)} %all-gather.7.cloned.1.call-done), kind=kOutput, calls=%fused_computation.21 | convolution fusion | flops 2147614720 | bytes 12845056 | tf_op jit(solution)/shard_map/dot_general | solution.py:51
  117.6 1.1 fusion.19
  118.7 73.8 %all-gather.9.cloned.1.call-done = bf16[256,64,128]{2,1,0:T(8,128)(2,1)} async-done(((bf16[8,64,128]{2,1,0:T(8,128)(2,1)}), bf16[256,64,128]{2,1,0:T(8,128)(2,1)}) %all-gather.9.cloned.1.call-update) | async-done | bytes 4194320 | tf_op jit(solution)/shard_map/all_gather | solution.py:13
  192.5 34.1 %while.40 = (s32[]{:T(128)}, f32[8,64,128]{2,1,0:T(8,128)S(1)}, s32[]{:T(128)}, bf16[32,8]{1,0:T(8,128)(2,1)S(1)}, bf16[32,8,64,128]{3,2,1,0:T(8,128)(2,1)}, /*index=5*/s32[]{:T(128)}, s32[]{:T(128)}, s32[]{:T(128)}, s32[]{:T(128)}) while((s32[]{:T(128)}, f32[8,64,128]{2,1,0:T(8,128)S(1)}, s32[]{:T(128)}, ...), condition=%wide.region_3.4_spmd.clone, body=%wide.region_2.3_spmd.clone.sunk | while | flops 327696 | bytes 655607 | solution.py:31
  216.0 1.0 fusion.61
  227.1 1.6 fusion.15
  228.7 1.0 convolution_bitcast_fusion.2
  231.4 43.4 %all-gather.11.cloned.1.call-done = bf16[256,64,128]{2,1,0:T(8,128)(2,1)} async-done(((bf16[8,64,128]{2,1,0:T(8,128)(2,1)}), bf16[256,64,128]{2,1,0:T(8,128)(2,1)}) %all-gather.11.cloned.1.call-update) | async-done | bytes 4194320 | tf_op jit(solution)/shard_map/all_gather | solution.py:13
  274.8 33.7 %while.41 = (s32[]{:T(128)}, f32[8,64,128]{2,1,0:T(8,128)S(1)}, s32[]{:T(128)}, bf16[32,8]{1,0:T(8,128)(2,1)S(1)}, bf16[32,8,64,128]{3,2,1,0:T(8,128)(2,1)}, /*index=5*/s32[]{:T(128)}, s32[]{:T(128)}) while((s32[]{:T(128)}, f32[8,64,128]{2,1,0:T(8,128)S(1)}, s32[]{:T(128)}, bf16[32,8]{1,0:T(8,128)(2,1)S(1)}, ...), condition=%wide.region_9.10_spmd.clone, body=%wide.region_8.9_spmd.clone.sunk | while | flops 327692 | bytes 655545 | solution.py:31
  308.5 1.0 convolution_bitcast_fusion.1
  310.6 7.8 %fusion.2 = bf16[8192,512]{0,1:T(8,128)(2,1)} fusion(bf16[256,512]{0,1:T(8,128)(2,1)S(1)} %bitcast.122, bf16[256,8192]{1,0:T(8,128)(2,1)} %param.10), kind=kOutput, calls=%fused_computation.7 | convolution fusion | flops 2151677952 | bytes 12845056 | tf_op jit(solution)/shard_map/dot_general | solution.py:101
  318.6 7.8 %convolution_convert_fusion.1 = bf16[256,8192]{1,0:T(8,128)(2,1)} fusion(bf16[256,512]{0,1:T(8,128)(2,1)S(1)} %bitcast.123, bf16[8192,512]{1,0:T(8,128)(2,1)} %all-gather.7.cloned.1.call-done), kind=kOutput, calls=%fused_computation.8 | convolution fusion | flops 2149580800 | bytes 12845056 | tf_op jit(solution)/shard_map/dot_general | solution.py:94
  326.4 47.2 %all-reduce.3.cloned.1.call-done = (bf16[256,128]{1,0:T(8,128)(2,1)}, bf16[256,128]{1,0:T(8,128)(2,1)}) async-done(((bf16[256,128]{1,0:T(8,128)(2,1)}, bf16[256,128]{1,0:T(8,128)(2,1)}), (bf16[256,128]{1,0:T(8,128)(2,1)}, bf16[256,128]{1,0:T(8,128)(2,1)})) %all-reduce.3.cloned.1.call-update) | async-done | bytes 131088 | tf_op jit(solution)/shard_map/psum | solution.py:91
  373.6 1.5 convert_element_type.131
  375.1 1.5 convert_element_type.135
  376.6 229.8 %reduce-scatter.5.cloned.1.call-done = bf16[256,512]{0,1:T(8,128)(2,1)} async-done(((bf16[8192,512]{0,1:T(8,128)(2,1)}), bf16[256,512]{0,1:T(8,128)(2,1)}) %reduce-scatter.5.cloned.1.call-update) | async-done | bytes 262160 | tf_op jit(solution)/shard_map/reduce_scatter | solution.py:100
  606.4 1.9 copy.39
  608.3 40.7 %reduce-scatter.3.cloned.1.call-done = bf16[256,1024]{1,0:T(8,128)(2,1)} async-done(((bf16[256,8192]{1,0:T(8,128)(2,1)}), bf16[256,1024]{1,0:T(8,128)(2,1)}) %reduce-scatter.3.cloned.1.call-update) | async-done | bytes 524304 | tf_op jit(solution)/shard_map/reduce_scatter | solution.py:97
  (162 shorter events, 69.7 us)
Async XLA Ops:
  7.2 47.5 %copy-start = (bf16[256,128]{1,0:T(8,128)(2,1)S(1)}, bf16[256,128]{1,0:T(8,128)(2,1)}, u32[]{:S(2)}) copy-start(bf16[256,128]{1,0:T(8,128)(2,1)} %param.13) | copy-start | bytes 196612
  7.2 103.3 %all-gather.7.cloned.1.call-start = ((), (), s32[]{:S(2)}) async-start(), calls=%async_computation.2 | async-start | bytes 8650752 | tf_op jit(solution)/shard_map/all_gather | solution.py:50
  7.9 184.6 %all-gather.9.cloned.1.call-start = ((), (), s32[]{:S(2)}) async-start(), calls=%async_computation.5 | async-start | bytes 4325376 | tf_op jit(solution)/shard_map/all_gather | solution.py:13
  12.7 262.1 %all-gather.11.cloned.1.call-start = ((), (), s32[]{:S(2)}) async-start(), calls=%async_computation.6 | async-start | bytes 4325376 | tf_op jit(solution)/shard_map/all_gather | solution.py:13
  118.7 254.9 %all-reduce.3.cloned.1.call-start = ((), (), s32[]{:S(2)}) async-start(), calls=%async_computation.7 | async-start | bytes 262144 | tf_op jit(solution)/shard_map/psum | solution.py:91
  226.6 3.8 copy-start.1
  310.5 295.9 %reduce-scatter.5.cloned.1.call-start = ((), (), s32[]{:S(2)}) async-start(), calls=%async_computation.4 | async-start | bytes 8650752 | tf_op jit(solution)/shard_map/reduce_scatter | solution.py:100
  318.4 330.7 %reduce-scatter.3.cloned.1.call-start = ((), (), s32[]{:S(2)}) async-start(), calls=%async_computation.3 | async-start | bytes 4718592 | tf_op jit(solution)/shard_map/reduce_scatter | solution.py:97
Sparse Core Ops, SparseCore 0:
  10.6 99.8 all-gather.6
  113.6 78.8 all-gather.8
  195.7 79.0 all-gather.10
  310.7 62.9 all-reduce.2
  378.0 228.3 reduce-scatter.4
  609.4 39.6 reduce-scatter.2
where the time goes:
time: 657 us; the launch traced here: 656 us
  waiting for transfers between devices  491 us (75%)
  other arithmetic  70.2 us (11%)
  blocking collectives  41.5 us (6%)
  matrix products  33.2 us (5%)
  between operations  14.3 us (2%)
    reduce_scatter x1, waiting for transfers between devices, per_device(): lax.psum_scatter(lax.dot_general(inputs, grad_values, (((0,), (0,)), ((),...  230 us
    all_gather x2, waiting for transfers between devices, carried_in(): lax.all_gather(part.astype(kind), axis)  117 us
    select_n x64, other arithmetic, lap(): return jax.tree.map(lambda a, b: jnp.where(reached, a, b), new, before)  64.8 us
    all_gather x1, waiting for transfers between devices, per_device(): w_full = lax.all_gather(w_value, 'seq', axis=0, tiled=True)  54.8 us
    psum x1, waiting for transfers between devices, per_device(): lax.psum(grad_b.reshape(steps, states).astype(jnp.bfloat16), 'head')  47.2 us
    all_gather x1, blocking collectives, carried_in(): lax.all_gather(part.astype(kind), axis)  41.5 us
    reduce_scatter x1, waiting for transfers between devices, per_device(): lax.psum_scatter(term.astype(jnp.bfloat16), 'head', scatter_dimension=1,...  40.7 us
  transfers between devices with their start and end apart: 6, of which 6 were waited for; matrix products, arithmetic and copies ran while one was open for 11% of the time, Pallas kernels for 0%

commit v1 on v0

--- a/solution.py
+++ b/solution.py
@@ -47,7 +47,9 @@
     depth = columns // heads
     states = b_proj.shape[1]
     blocks = steps // SPAN
-    w_full = lax.all_gather(w_value, "seq", axis=0, tiled=True)
+    w_full = jnp.concatenate(
+        lax.all_to_all(jnp.stack([w_value] * lax.axis_size("seq")), "seq", 0, 0), axis=0
+    )
     values = jnp.dot(inputs, w_full, preferred_element_type=jnp.float32).astype(jnp.bfloat16)
     xs = values.astype(jnp.float32).reshape(blocks, SPAN, heads, depth)
     dys = grad_out.astype(jnp.float32).reshape(blocks, SPAN, heads, depth)

time: 657 us -> 734 us (1.12)
  blocking collectives: 41.5 us -> 238 us
  waiting for transfers between devices: 491 us -> 358 us
  starting transfers between devices: 0.42 us -> 12.3 us
    all_gather x1, blocking collectives: 41.5 us -> 238 us  [carried_in(): lax.all_gather(part.astype(kind), axis)]
    all_gather x2, waiting for transfers between devices: 117 us -> 39.9 us  [carried_in(): lax.all_gather(part.astype(kind), axis)]
    all_gather x1 -> x0, waiting for transfers between devices: 54.8 us -> none  [per_device(): w_full = lax.all_gather(w_value, 'seq', axis=0, tiled=True)]
    all_to_all x0 -> x1, starting transfers between devices: none -> 11.9 us  [per_device(): lax.all_to_all(jnp.stack([w_value] * lax.axis_size('seq')), 'seq', 0, 0)]
  transfers between devices with their start and end apart: 6 -> 6, of which waited for: 6 -> 4; matrix products, arithmetic and copies ran while one was open for 11% -> 9% of each run, Pallas kernels for 0% -> 0%
where the time goes in v1:
time: 734 us; the launch traced here: 733 us
  waiting for transfers between devices  358 us (49%)
  blocking collectives  238 us (32%)
  other arithmetic  69.5 us (9%)
  matrix products  31.6 us (4%)
  between operations  13.9 us (2%)
  starting transfers between devices  12.3 us (2%)
  local copies, waits for them, and re-layouts  7.77 us (1%)
    all_gather x1, blocking collectives, carried_in(): lax.all_gather(part.astype(kind), axis)  238 us
    reduce_scatter x1, waiting for transfers between devices, per_device(): lax.psum_scatter(lax.dot_general(inputs, grad_values, (((0,), (0,)), ((),...  230 us
    select_n x64, other arithmetic, lap(): return jax.tree.map(lambda a, b: jnp.where(reached, a, b), new, before)  64.9 us
    psum x1, waiting for transfers between devices, per_device(): lax.psum(grad_b.reshape(steps, states).astype(jnp.bfloat16), 'head')  47.2 us
    reduce_scatter x1, waiting for transfers between devices, per_device(): lax.psum_scatter(term.astype(jnp.bfloat16), 'head', scatter_dimension=1,...  40.8 us
    all_gather x2, waiting for transfers between devices, carried_in(): lax.all_gather(part.astype(kind), axis)  39.9 us
  transfers between devices with their start and end apart: 6, of which 4 were waited for; matrix products, arithmetic and copies ran while one was open for 9% of the time, Pallas kernels for 0%

profile of v1, /device:TPU:8, one launch (start us, length us, event | category | flops | bytes accessed | tf_op | source)
XLA Modules:
  0.0 732.7 jit_solution(10546251889988314916)
XLA Ops:
  7.2 5.2 stack.2
  12.3 11.9 %all-to-all-start = ((bf16[32,256,512]{2,1,0:T(8,128)(2,1)}), bf16[32,256,512]{2,1,0:T(8,128)(2,1)}, u32[]{:S(2)}, u32[]{:S(2)}) async-start(bf16[32,256,512]{2,1,0:T(8,128)(2,1)} %stack.2), calls=%async_computation | async-start | bytes 16777216 | tf_op jit(solution)/shard_map/all_to_all | solution.py:51
  25.5 1.1 fusion.18
  26.8 237.6 %all-gather = bf16[32,1,8]{2,1,0:T(2,128)(2,1)S(1)} all-gather(bf16[1,1,8]{2,1,0:T(2,128)(2,1)S(1)} %copy.34), channel_id=2, replica_groups=mesh['seq'=32,'head'=8] {'seq'}, dimensions={0}, use_global_device_ids=true | all-gather | bytes 528 | tf_op jit(solution)/shard_map/all_gather | solution.py:13
  264.8 7.0 convolution_convert_fusion.2
  271.9 1.1 fusion.19
  273.1 34.2 %while.40 = (s32[]{:T(128)}, f32[8,64,128]{2,1,0:T(8,128)S(1)}, s32[]{:T(128)}, bf16[32,8]{1,0:T(8,128)(2,1)S(1)}, bf16[32,8,64,128]{3,2,1,0:T(8,128)(2,1)}, /*index=5*/s32[]{:T(128)}, s32[]{:T(128)}, s32[]{:T(128)}, s32[]{:T(128)}) while((s32[]{:T(128)}, f32[8,64,128]{2,1,0:T(8,128)S(1)}, s32[]{:T(128)}, ...), condition=%wide.region_3.4_spmd.clone, body=%wide.region_2.3_spmd.clone.sunk | while | flops 327696 | bytes 655607 | solution.py:31
  282.8 1.0 fusion.61
  296.6 1.0 fusion.61
  299.8 1.0 fusion.61
  307.7 1.6 fusion.15
  309.3 1.0 convolution_bitcast_fusion.2
  312.0 39.9 %all-gather.8.cloned.1.call-done = bf16[256,64,128]{2,1,0:T(8,128)(2,1)} async-done(((bf16[8,64,128]{2,1,0:T(8,128)(2,1)}), bf16[256,64,128]{2,1,0:T(8,128)(2,1)}) %all-gather.8.cloned.1.call-update) | async-done | bytes 4194320 | tf_op jit(solution)/shard_map/all_gather | solution.py:13
  351.9 33.7 %while.41 = (s32[]{:T(128)}, f32[8,64,128]{2,1,0:T(8,128)S(1)}, s32[]{:T(128)}, bf16[32,8]{1,0:T(8,128)(2,1)S(1)}, bf16[32,8,64,128]{3,2,1,0:T(8,128)(2,1)}, /*index=5*/s32[]{:T(128)}, s32[]{:T(128)}) while((s32[]{:T(128)}, f32[8,64,128]{2,1,0:T(8,128)S(1)}, s32[]{:T(128)}, bf16[32,8]{1,0:T(8,128)(2,1)S(1)}, ...), condition=%wide.region_9.10_spmd.clone, body=%wide.region_8.9_spmd.clone.sunk | while | flops 327692 | bytes 655545 | solution.py:31
  385.6 1.0 convolution_bitcast_fusion.1
  386.6 1.0 fusion.21
  387.9 7.8 %fusion.2 = bf16[8192,512]{0,1:T(8,128)(2,1)} fusion(bf16[256,512]{0,1:T(8,128)(2,1)S(1)} %bitcast.123, bf16[256,8192]{1,0:T(8,128)(2,1)} %param.10), kind=kOutput, calls=%fused_computation.7 | convolution fusion | flops 2151677952 | bytes 12845056 | tf_op jit(solution)/shard_map/dot_general | solution.py:103
  395.7 7.8 %convolution_convert_fusion.1 = bf16[256,8192]{1,0:T(8,128)(2,1)} fusion(bf16[256,512]{0,1:T(8,128)(2,1)S(1)} %bitcast.124, bf16[8192,512]{1,0:T(8,128)(2,1)} %bitcast.23), kind=kOutput, calls=%fused_computation.8 | convolution fusion | flops 2149580800 | bytes 12845056 | tf_op jit(solution)/shard_map/dot_general | solution.py:96
  403.5 47.2 %all-reduce.3.cloned.1.call-done = (bf16[256,128]{1,0:T(8,128)(2,1)}, bf16[256,128]{1,0:T(8,128)(2,1)}) async-done(((bf16[256,128]{1,0:T(8,128)(2,1)}, bf16[256,128]{1,0:T(8,128)(2,1)}), (bf16[256,128]{1,0:T(8,128)(2,1)}, bf16[256,128]{1,0:T(8,128)(2,1)})) %all-reduce.3.cloned.1.call-update) | async-done | bytes 131088 | tf_op jit(solution)/shard_map/psum | solution.py:93
  450.7 1.5 convert_element_type.132
  452.2 1.5 convert_element_type.136
  453.7 229.8 %reduce-scatter.5.cloned.1.call-done = bf16[256,512]{0,1:T(8,128)(2,1)} async-done(((bf16[8192,512]{0,1:T(8,128)(2,1)}), bf16[256,512]{0,1:T(8,128)(2,1)}) %reduce-scatter.5.cloned.1.call-update) | async-done | bytes 262160 | tf_op jit(solution)/shard_map/reduce_scatter | solution.py:102
  683.5 1.9 copy.39
  685.4 40.8 %reduce-scatter.3.cloned.1.call-done = bf16[256,1024]{1,0:T(8,128)(2,1)} async-done(((bf16[256,8192]{1,0:T(8,128)(2,1)}), bf16[256,1024]{1,0:T(8,128)(2,1)}) %reduce-scatter.3.cloned.1.call-update) | async-done | bytes 524304 | tf_op jit(solution)/shard_map/reduce_scatter | solution.py:99
  (166 shorter events, 66.9 us)
Async XLA Ops:
  7.2 257.5 %copy-start = (bf16[256,128]{1,0:T(8,128)(2,1)S(1)}, bf16[256,128]{1,0:T(8,128)(2,1)}, u32[]{:S(2)}) copy-start(bf16[256,128]{1,0:T(8,128)(2,1)} %param.13) | copy-start | bytes 196612
  12.3 12.0 %copy-start.3 = (f32[256,8]{0,1:T(8,128)S(1)}, f32[256,8]{0,1:T(8,128)}, u32[]{:S(2)}) copy-start(f32[256,8]{0,1:T(8,128)} %param.12) | copy-start | bytes 24580
  12.3 12.7 %copy-start.2 = (bf16[256,512]{1,0:T(8,128)(2,1)S(1)}, bf16[256,512]{1,0:T(8,128)(2,1)}, u32[]{:S(2)}) copy-start(bf16[256,512]{1,0:T(8,128)(2,1)} %param.15) | copy-start | bytes 786436
  12.3 13.2 %copy-start.1 = (bf16[256,128]{1,0:T(8,128)(2,1)S(1)}, bf16[256,128]{1,0:T(8,128)(2,1)}, u32[]{:S(2)}) copy-start(bf16[256,128]{1,0:T(8,128)(2,1)} %param.14) | copy-start | bytes 196612
  12.3 252.5 %all-to-all-start = ((bf16[32,256,512]{2,1,0:T(8,128)(2,1)}), bf16[32,256,512]{2,1,0:T(8,128)(2,1)}, u32[]{:S(2)}, u32[]{:S(2)}) async-start(bf16[32,256,512]{2,1,0:T(8,128)(2,1)} %stack.2), calls=%async_computation | async-start | bytes 16777216 | tf_op jit(solution)/shard_map/all_to_all | solution.py:51
  24.2 248.9 %all-gather.6.cloned.1.call-start = ((), (), s32[]{:S(2)}) async-start(), calls=%async_computation.5 | async-start | bytes 4325376 | tf_op jit(solution)/shard_map/all_gather | solution.py:13
  26.6 325.3 %all-gather.8.cloned.1.call-start = ((), (), s32[]{:S(2)}) async-start(), calls=%async_computation.6 | async-start | bytes 4325376 | tf_op jit(solution)/shard_map/all_gather | solution.py:13
  273.0 177.7 %all-reduce.3.cloned.1.call-start = ((), (), s32[]{:S(2)}) async-start(), calls=%async_computation.7 | async-start | bytes 262144 | tf_op jit(solution)/shard_map/psum | solution.py:93
  387.6 295.8 %reduce-scatter.5.cloned.1.call-start = ((), (), s32[]{:S(2)}) async-start(), calls=%async_computation.4 | async-start | bytes 8650752 | tf_op jit(solution)/shard_map/reduce_scatter | solution.py:102
  395.7 330.5 %reduce-scatter.3.cloned.1.call-start = ((), (), s32[]{:S(2)}) async-start(), calls=%async_computation.3 | async-start | bytes 4718592 | tf_op jit(solution)/shard_map/reduce_scatter | solution.py:99
Sparse Core Ops, SparseCore 0:
  28.2 141.5 all-gather.5
  273.2 78.6 all-gather.7
  387.8 62.9 all-reduce.2
  455.1 228.3 reduce-scatter.4
  686.5 39.6 reduce-scatter.2
